TPU v7x, 256 devices: a whole 4x4x8 slice. The times are simulated.
256 devices in a mesh: dom: 64 (over z, y, core), grp: 4 (over x).
Axes of the slice: x: 4, y: 4, z: 8, core: 2. Of those that a mesh axis runs over, the one named last changes fastest.
Arguments:
- features: bfloat16 [4, 65536, 512], P('grp', 'dom'), may hold values from -6 to 6
- history: bfloat16 [2, 4, 65536, 512], P(None, 'grp', 'dom'), may hold values from -6 to 6
- adj_tiles: bfloat16 [4, 512, 4, 128, 128], P('grp', 'dom'), may hold values from -0.25 to 0.25
- blocks: int32 [4, 512, 4], P('grp', 'dom'), may hold values from 0 to 11, as said below
- send_list: int32 [4, 64, 64, 8], P('grp', 'dom'), may hold values from 0 to 1023
- counts: int32 [4, 64, 64], P('grp', 'dom'), may hold values from 0 to 8, as said below
- weights: bfloat16 [3, 512, 512], replicated, may hold values from -0.25 to 0.25
- cotangent: bfloat16 [4, 65536, 512], P('grp', 'dom'), may hold values from -16 to 16
Outputs:
- embedding: bfloat16 [4, 65536, 512], P('grp', 'dom')
- fresh_halo: bfloat16 [2, 4, 32768, 512], P(None, 'grp', 'dom')
- weight_grads: float32 [3, 512, 512], P(None, 'dom')
Inputs may be any that keep to these rules, and one draw needn't show every extreme that they name: `send_list`: entries at or past counts are not read. counts[g, q, p] is zero where q equals p; some owner uses all 8 slots for every other partition, and some partition gets 8 rows from every other owner. Entry 0 of the list of a partition's block b is b itself; entries 2 and 3 name halo blocks, at least 8.
All inputs are finite; a program needn't handle non-finite values.
Results may differ from a plain program's by a relative error of at most 0.012.
Values may be sent and summed in bfloat16 or wider, within the bound.
A program may use at most 128 MiB of HBM per device.

v0:
```python
import math
import jax
import jax.numpy as jnp
from jax import lax
from jax.sharding import PartitionSpec as P


def silu_slope(values):
    sigmoid_part = jax.nn.sigmoid(values)
    return sigmoid_part * (1.0 + values * (1.0 - sigmoid_part))


def pack_rows(source_rows, send_rows, live_counts):
    peer_count = send_rows.shape[0]
    capacity = send_rows.shape[1]
    picked = jnp.take(source_rows, send_rows.reshape(-1), axis=0)
    picked = picked.reshape(peer_count, capacity, source_rows.shape[1])
    in_use = jnp.arange(capacity, dtype=jnp.int32)[None, :] < live_counts[:, None]
    return jnp.where(in_use[:, :, None], picked, jnp.zeros((), jnp.bfloat16))


def aggregate(local_rows, halo_rows, tile_set, block_set):
    block_rows = tile_set.shape[-1]
    row_width = local_rows.shape[1]
    source = jnp.concatenate([local_rows, halo_rows], axis=0).reshape(-1, block_rows, row_width)
    picked = jnp.take(source, block_set.reshape(-1), axis=0)
    picked = picked.reshape(block_set.shape + (block_rows, row_width))
    mixed = jnp.einsum("bkij,bkjd->bid", tile_set, picked, preferred_element_type=jnp.float32)
    return mixed.reshape(-1, row_width)


def spread_back(grad_rows, tile_set, block_set):
    block_rows = tile_set.shape[-1]
    row_width = grad_rows.shape[1]
    local_blocks = grad_rows.shape[0] // block_rows
    by_block = grad_rows.reshape(-1, block_rows, row_width)
    contrib_terms = jnp.einsum(
        "bkij,bid->bkjd", tile_set, by_block, preferred_element_type=jnp.float32
    )
    owners = (
        block_set.reshape(1, -1) == jnp.arange(local_blocks, dtype=jnp.int32)[:, None]
    ).astype(jnp.float32)
    summed = jnp.dot(
        owners,
        contrib_terms.reshape(owners.shape[1], -1),
        precision=lax.Precision.HIGHEST,
        preferred_element_type=jnp.float32,
    )
    return summed.reshape(-1, row_width)


def body(features, history, adj_tiles, blocks, send_list, counts, weights, cotangent):
    node_rows = features[0]
    tile_set = adj_tiles[0]
    block_set = blocks[0]
    send_rows = send_list[0, 0]
    live_counts = counts[0, 0]
    row_width = node_rows.shape[1]
    pulled = (
        lax.all_to_all(
            pack_rows(node_rows, send_rows, live_counts),
            "dom",
            split_axis=0,
            concat_axis=0,
            tiled=True,
        ),
        lax.all_to_all(
            pack_rows(history[0, 0], send_rows, live_counts),
            "dom",
            split_axis=0,
            concat_axis=0,
            tiled=True,
        ),
        lax.all_to_all(
            pack_rows(history[1, 0], send_rows, live_counts),
            "dom",
            split_axis=0,
            concat_axis=0,
            tiled=True,
        ),
    )
    halo_inputs = [piece.reshape(-1, row_width) for piece in pulled]
    current = node_rows
    aggregated = []
    linear_out = []
    hidden_rows = []
    fresh_parts = []
    for layer_index in range(3):
        mixed = aggregate(current, halo_inputs[layer_index], tile_set, block_set).astype(
            jnp.bfloat16
        )
        product = jnp.dot(mixed, weights[layer_index], preferred_element_type=jnp.float32)
        aggregated.append(mixed)
        linear_out.append(product)
        if layer_index < 2:
            current = jax.nn.silu(product).astype(jnp.bfloat16)
            hidden_rows.append(current)
    node_out = linear_out[2].astype(jnp.bfloat16)
    fresh_parts = list(
        (
            lax.all_to_all(
                pack_rows(hidden_rows[0], send_rows, live_counts),
                "dom",
                split_axis=0,
                concat_axis=0,
                tiled=True,
            ),
            lax.all_to_all(
                pack_rows(hidden_rows[1], send_rows, live_counts),
                "dom",
                split_axis=0,
                concat_axis=0,
                tiled=True,
            ),
        )
    )
    fresh_halo = jnp.stack([piece.reshape(-1, row_width) for piece in fresh_parts])
    upstream = cotangent[0]
    partial_sums = [None, None, None]
    for layer_index in (2, 1, 0):
        partial_sums[layer_index] = lax.dot_general(
            aggregated[layer_index],
            upstream,
            (((0,), (0,)), ((), ())),
            preferred_element_type=jnp.float32,
        )
        if layer_index > 0:
            slope_in = lax.dot_general(
                upstream,
                weights[layer_index],
                (((1,), (1,)), ((), ())),
                preferred_element_type=jnp.float32,
            ).astype(jnp.bfloat16)
            back_rows = spread_back(slope_in, tile_set, block_set)
            upstream = (back_rows * silu_slope(linear_out[layer_index - 1])).astype(jnp.bfloat16)
    total_rows = lax.axis_size("grp") * lax.axis_size("dom") * node_rows.shape[0]
    stacked = jnp.stack(partial_sums) * (1.0 / math.sqrt(total_rows))
    replica_total = lax.psum(stacked.astype(jnp.bfloat16), "grp").astype(jnp.float32)
    weight_grads = lax.psum_scatter(replica_total, "dom", scatter_dimension=1, tiled=True)
    return (node_out[None], fresh_halo[:, None], weight_grads)


def solution(mesh):
    placed = (
        P("grp", "dom", None),
        P(None, "grp", "dom", None),
        P("grp", "dom", None, None, None),
        P("grp", "dom", None),
        P("grp", "dom", None, None),
        P("grp", "dom", None),
        P(),
        P("grp", "dom", None),
    )
    return jax.shard_map(
        body,
        mesh=mesh,
        in_specs=placed,
        out_specs=(P("grp", "dom", None), P(None, "grp", "dom", None), P(None, "dom", None)),
        check_vma=False,
    )
```

profile of v0, /device:TPU:2, one launch (start us, length us, event | category | flops | bytes accessed | tf_op | source)
XLA Modules:
  0.0 374.4 jit_solution(13997142385125871676)
XLA Ops:
  8.9 3.3 gather_fusion
  13.3 12.4 %all-to-all-start = ((bf16[64,8,512]{2,1,0:T(8,128)(2,1)}), bf16[64,8,512]{2,1,0:T(8,128)(2,1)}, u32[]{:S(2)}, u32[]{:S(2)}) async-start(bf16[64,8,512]{2,1,0:T(8,128)(2,1)} %bitcast_select_fusion.4), calls=%async_computation | async-start | bytes 1048576 | tf_op jit(solution)/shard_map/all_to_all | solution.py:60
  27.5 2.6 gather_fusion.2
  30.1 2.6 gather_fusion.4
  32.8 10.3 %all-to-all-done = bf16[64,8,512]{2,1,0:T(8,128)(2,1)} async-done(((bf16[64,8,512]{2,1,0:T(8,128)(2,1)}), bf16[64,8,512]{2,1,0:T(8,128)(2,1)}, u32[]{:S(2)}, u32[]{:S(2)}) %all-to-all-start) | async-done | bytes 524320 | tf_op jit(solution)/shard_map/all_to_all | solution.py:60
  45.4 4.2 %gather_fusion.1 = bf16[32,128,512]{2,1,0:T(8,128)(2,1)} fusion(bf16[12,128,512]{2,1,0:T(8,128)(2,1)} %bitcast.138, s32[1024]{0:T(1024)S(1)} %pad_clamp_fusion), kind=kCustom, calls=%fused_computation.1.clone | custom fusion | bytes 8388736 | tf_op jit(solution)/shard_map/jit(_take)/gather | solution.py:26
  49.6 2.6 broadcast_select_fusion
  53.0 3.7 multiply_convert_fusion.3
  56.7 2.6 gather_fusion.6
  61.8 5.9 %all-to-all-start.1 = ((bf16[64,8,512]{2,1,0:T(8,128)(2,1)}), bf16[64,8,512]{2,1,0:T(8,128)(2,1)S(1)}, u32[]{:S(2)}, u32[]{:S(2)}) async-start(bf16[64,8,512]{2,1,0:T(8,128)(2,1)} %get-tuple-element.10), calls=%async_computation.1 | async-start | bytes 1048576 | tf_op jit(solution)/shard_map/all_to_all | solution.py:67
  69.8 4.5 %convolution_bitcast_fusion.1 = f32[8,4,128,512]{2,3,1,0:T(8,128)} fusion(bf16[8,128,512,1]{2,1,3,0:T(8,128)(2,1)S(1)} %bitcast.150, bf16[1,8,4,128,128]{4,3,2,1,0:T(8,128)(2,1)S(1)} %copy-done), kind=kOutput, calls=%fused_computation.12 | convolution fusion | flops 536870912 | bytes 10485760 | tf_op jit(solution)/shard_map/bkij,bid->bkjd/dot_general | solution.py:37
  74.3 10.4 %copy.29 = f32[4,8,128,512]{3,1,2,0:T(8,128)} copy(f32[4,8,128,512]{2,3,1,0:T(8,128)} %bitcast.127) | data formatting | bytes 16777216
  84.7 7.5 %fusion.22 = f32[8,65536]{1,0:T(8,128)} fusion(f32[32,65536]{1,0:T(8,128)} %bitcast.130, s32[32]{0:T(128)S(1)} %reshape_squeeze.5), kind=kOutput, calls=%fused_computation.67 | convolution fusion | flops 201326848 | bytes 10485888 | tf_op jit(solution)/shard_map/dot_general | solution.py:43
  92.2 3.3 reshape.126
  95.5 10.1 %all-to-all-start.2 = ((bf16[64,8,512]{2,1,0:T(8,128)(2,1)}), bf16[64,8,512]{2,1,0:T(8,128)(2,1)S(1)}, u32[]{:S(2)}, u32[]{:S(2)}) async-start(bf16[64,8,512]{2,1,0:T(8,128)(2,1)} %get-tuple-element.11), calls=%async_computation.2 | async-start | bytes 1048576 | tf_op jit(solution)/shard_map/all_to_all | solution.py:74
  107.2 4.2 %gather_fusion.3 = bf16[32,128,512]{2,1,0:T(8,128)(2,1)} fusion(bf16[12,128,512]{2,1,0:T(8,128)(2,1)} %bitcast.136, s32[1024]{0:T(1024)S(1)} %pad_clamp_fusion), kind=kCustom, calls=%fused_computation.6.clone | custom fusion | bytes 8388736 | tf_op jit(solution)/shard_map/jit(_take)/gather | solution.py:26
  111.4 2.6 broadcast_select_fusion.1
  124.6 4.2 %gather_fusion.5 = bf16[32,128,512]{2,1,0:T(8,128)(2,1)} fusion(bf16[12,128,512]{2,1,0:T(8,128)(2,1)} %bitcast.137, s32[1024]{0:T(1024)S(1)} %pad_clamp_fusion), kind=kCustom, calls=%fused_computation.7.clone | custom fusion | bytes 8388736 | tf_op jit(solution)/shard_map/jit(_take)/gather | solution.py:26
  128.7 2.6 broadcast_select_fusion.2
  134.3 4.5 %convolution_bitcast_fusion = f32[8,4,128,512]{2,3,1,0:T(8,128)} fusion(bf16[8,128,512,1]{2,1,3,0:T(8,128)(2,1)S(1)} %bitcast.149, bf16[1,8,4,128,128]{4,3,2,1,0:T(8,128)(2,1)S(1)} %copy-done), kind=kOutput, calls=%fused_computation.11 | convolution fusion | flops 536870912 | bytes 10485760 | tf_op jit(solution)/shard_map/bkij,bid->bkjd/dot_general | solution.py:37
  138.9 10.4 %copy.30 = f32[4,8,128,512]{3,1,2,0:T(8,128)} copy(f32[4,8,128,512]{2,3,1,0:T(8,128)} %bitcast.128) | data formatting | bytes 16777216
  149.2 7.5 %fusion.21 = f32[8,65536]{1,0:T(8,128)} fusion(f32[32,65536]{1,0:T(8,128)} %bitcast.129, s32[32]{0:T(128)S(1)} %reshape_squeeze.5), kind=kOutput, calls=%fused_computation.66 | convolution fusion | flops 201326848 | bytes 10485888 | tf_op jit(solution)/shard_map/dot_general | solution.py:43
  156.8 3.4 reshape.129
  160.2 3.5 convolution_bitcast_fusion.4
  165.4 53.3 %all-reduce.2.cloned.1.call-done = bf16[3,512,512]{2,1,0:T(8,128)(2,1)} async-done(((bf16[3,512,512]{2,1,0:T(8,128)(2,1)}), bf16[3,512,512]{2,1,0:T(8,128)(2,1)}) %all-reduce.2.cloned.1.call-update) | async-done | bytes 1572880 | tf_op jit(solution)/shard_map/psum | solution.py:138
  218.7 3.5 convert_element_type.78
  222.2 10.7 %all-to-all-start.3 = ((bf16[64,8,512]{2,1,0:T(8,128)(2,1)}), bf16[64,8,512]{2,1,0:T(8,128)(2,1)S(1)}, u32[]{:S(2)}, u32[]{:S(2)}) async-start(bf16[64,8,512]{2,1,0:T(8,128)(2,1)} %get-tuple-element.9), calls=%async_computation.3 | async-start | bytes 1048576 | tf_op jit(solution)/shard_map/all_to_all | solution.py:101
  235.9 14.6 %all-to-all-done.3 = bf16[64,8,512]{2,1,0:T(8,128)(2,1)S(1)} async-done(((bf16[64,8,512]{2,1,0:T(8,128)(2,1)}), bf16[64,8,512]{2,1,0:T(8,128)(2,1)S(1)}, u32[]{:S(2)}, u32[]{:S(2)}) %all-to-all-start.3) | async-done | bytes 524320 | tf_op jit(solution)/shard_map/all_to_all | solution.py:101
  250.6 5.8 %all-to-all-start.4 = ((bf16[64,8,512]{2,1,0:T(8,128)(2,1)}), bf16[64,8,512]{2,1,0:T(8,128)(2,1)S(1)}, u32[]{:S(2)}, u32[]{:S(2)}) async-start(bf16[64,8,512]{2,1,0:T(8,128)(2,1)} %bitcast_select_fusion), calls=%async_computation.4 | async-start | bytes 1048576 | tf_op jit(solution)/shard_map/all_to_all | solution.py:108
  256.3 3.1 fusion.1
  259.4 14.6 %all-to-all-done.4 = bf16[64,8,512]{2,1,0:T(8,128)(2,1)S(1)} async-done(((bf16[64,8,512]{2,1,0:T(8,128)(2,1)}), bf16[64,8,512]{2,1,0:T(8,128)(2,1)S(1)}, u32[]{:S(2)}, u32[]{:S(2)}) %all-to-all-start.4) | async-done | bytes 524320 | tf_op jit(solution)/shard_map/all_to_all | solution.py:108
  275.0 92.5 %reduce-scatter.2.cloned.1.call-done = f32[3,8,512]{2,1,0:T(8,128)} async-done(((f32[3,512,512]{2,1,0:T(8,128)}), f32[3,8,512]{2,1,0:T(8,128)}) %reduce-scatter.2.cloned.1.call-update) | async-done | bytes 49168 | tf_op jit(solution)/shard_map/reduce_scatter | solution.py:139
  (63 shorter events, 32.9 us)
Async XLA Ops:
  7.2 45.1 %copy-start = (bf16[1,8,4,128,128]{4,3,2,1,0:T(8,128)(2,1)S(1)}, bf16[1,8,4,128,128]{4,3,2,1,0:T(8,128)(2,1)}, u32[]{:S(2)}) copy-start(bf16[1,8,4,128,128]{4,3,2,1,0:T(8,128)(2,1)} %param.14) | copy-start | bytes 3145732
  12.3 13.4 %copy-start.11 = (s32[1,8,4]{1,2,0:T(4,128)S(1)}, s32[1,8,4]{1,2,0:T(4,128)}, u32[]{:S(2)}) copy-start(s32[1,8,4]{1,2,0:T(4,128)} %param.15) | copy-start | bytes 388
  13.3 29.8 %all-to-all-start = ((bf16[64,8,512]{2,1,0:T(8,128)(2,1)}), bf16[64,8,512]{2,1,0:T(8,128)(2,1)}, u32[]{:S(2)}, u32[]{:S(2)}) async-start(bf16[64,8,512]{2,1,0:T(8,128)(2,1)} %bitcast_select_fusion.4), calls=%async_computation | async-start | bytes 1048576 | tf_op jit(solution)/shard_map/all_to_all | solution.py:60
  30.1 13.0 %copy-start.1 = (bf16[1,1024,512]{2,1,0:T(8,128)(2,1)S(1)}, bf16[1,1024,512]{2,1,0:T(8,128)(2,1)}, u32[]{:S(2)}) copy-start(bf16[1,1024,512]{2,1,0:T(8,128)(2,1)} %param.12) | copy-start | bytes 3145732
  53.0 3.7 copy-start.5
  56.7 2.6 copy-start.3
  56.7 2.6 copy-start.4
  61.8 33.8 %all-to-all-start.1 = ((bf16[64,8,512]{2,1,0:T(8,128)(2,1)}), bf16[64,8,512]{2,1,0:T(8,128)(2,1)S(1)}, u32[]{:S(2)}, u32[]{:S(2)}) async-start(bf16[64,8,512]{2,1,0:T(8,128)(2,1)} %get-tuple-element.10), calls=%async_computation.1 | async-start | bytes 1048576 | tf_op jit(solution)/shard_map/all_to_all | solution.py:67
  95.5 27.8 %all-to-all-start.2 = ((bf16[64,8,512]{2,1,0:T(8,128)(2,1)}), bf16[64,8,512]{2,1,0:T(8,128)(2,1)S(1)}, u32[]{:S(2)}, u32[]{:S(2)}) async-start(bf16[64,8,512]{2,1,0:T(8,128)(2,1)} %get-tuple-element.11), calls=%async_computation.2 | async-start | bytes 1048576 | tf_op jit(solution)/shard_map/all_to_all | solution.py:74
  105.7 113.0 %all-reduce.2.cloned.1.call-start = ((), (), s32[]{:S(2)}) async-start(), calls=%async_computation.6 | async-start | bytes 3145728 | tf_op jit(solution)/shard_map/psum | solution.py:138
  114.0 1.6 copy-start.2
  114.0 2.0 copy-start.12
  131.4 1.2 copy-start.13
  132.2 2.2 copy-start.7
  132.6 1.7 copy-start.8
  156.8 3.4 copy-start.6
  160.2 3.5 copy-start.9
  160.2 3.5 copy-start.10
  165.3 202.2 %reduce-scatter.2.cloned.1.call-start = ((), (), s32[]{:S(2)}) async-start(), calls=%async_computation.7 | async-start | bytes 3194880 | tf_op jit(solution)/shard_map/reduce_scatter | solution.py:139
  222.2 28.4 %all-to-all-start.3 = ((bf16[64,8,512]{2,1,0:T(8,128)(2,1)}), bf16[64,8,512]{2,1,0:T(8,128)(2,1)S(1)}, u32[]{:S(2)}, u32[]{:S(2)}) async-start(bf16[64,8,512]{2,1,0:T(8,128)(2,1)} %get-tuple-element.9), calls=%async_computation.3 | async-start | bytes 1048576 | tf_op jit(solution)/shard_map/all_to_all | solution.py:101
  250.6 23.4 %all-to-all-start.4 = ((bf16[64,8,512]{2,1,0:T(8,128)(2,1)}), bf16[64,8,512]{2,1,0:T(8,128)(2,1)S(1)}, u32[]{:S(2)}, u32[]{:S(2)}) async-start(bf16[64,8,512]{2,1,0:T(8,128)(2,1)} %bitcast_select_fusion), calls=%async_computation.4 | async-start | bytes 1048576 | tf_op jit(solution)/shard_map/all_to_all | solution.py:108
Sparse Core Ops, SparseCore 0:
  165.4 53.2 all-reduce.1
  223.4 144.1 reduce-scatter.1
where the time goes:
time: 376 us; the launch traced here: 374 us
  waiting for transfers between devices  188 us (50%)
  local copies, waits for them, and re-layouts  57.8 us (15%)
  starting transfers between devices  45.2 us (12%)
  matrix products  45.1 us (12%)
  other arithmetic  24.2 us (6%)
  between operations  14.3 us (4%)
    reduce_scatter x1, waiting for transfers between devices, body(): lax.psum_scatter(replica_total, 'dom', scatter_dimension=1, tiled=True)  92.5 us
    psum x1, waiting for transfers between devices, body(): lax.psum(stacked.astype(jnp.bfloat16), 'grp').astype(jnp.float32)  53.3 us
    unnamed x32, local copies, waits for them, and re-layouts  23.5 us
    dot_general x2, matrix products, spread_back(): jnp.dot(owners, contrib_terms.reshape(owners.shape[1], -1), precision=lax...  15 us
    all_to_all x1, waiting for transfers between devices, body(): lax.all_to_all(pack_rows(hidden_rows[0], send_rows, live_counts), 'dom',...  14.6 us
    all_to_all x1, waiting for transfers between devices, body(): lax.all_to_all(pack_rows(hidden_rows[1], send_rows, live_counts), 'dom',...  14.6 us
    gather x5, local copies, waits for them, and re-layouts, pack_rows(): picked = jnp.take(source_rows, send_rows.reshape(-1), axis=0)  13.2 us
    gather x3, local copies, waits for them, and re-layouts, aggregate(): picked = jnp.take(source, block_set.reshape(-1), axis=0)  12.5 us
  transfers between devices with their start and end apart: 7, of which 6 were waited for; matrix products, arithmetic and copies ran while one was open for 15% of the time, Pallas kernels for 0%

commit v1 on v0

--- a/solution.py
+++ b/solution.py
@@ -135,7 +135,9 @@
             upstream = (back_rows * silu_slope(linear_out[layer_index - 1])).astype(jnp.bfloat16)
     total_rows = lax.axis_size("grp") * lax.axis_size("dom") * node_rows.shape[0]
     stacked = jnp.stack(partial_sums) * (1.0 / math.sqrt(total_rows))
-    replica_total = lax.psum(stacked.astype(jnp.bfloat16), "grp").astype(jnp.float32)
+    replica_total = jnp.sum(lax.all_gather(stacked.astype(jnp.bfloat16), "grp"), axis=0).astype(
+        jnp.float32
+    )
     weight_grads = lax.psum_scatter(replica_total, "dom", scatter_dimension=1, tiled=True)
     return (node_out[None], fresh_halo[:, None], weight_grads)
 

time: 376 us -> 394 us (1.048)
  waiting for transfers between devices: 188 us -> 200 us
  other arithmetic: 24.2 us -> 29.6 us
    all_gather x0 -> x1, waiting for transfers between devices: none -> 66.5 us  [body(): lax.all_gather(stacked.astype(jnp.bfloat16), 'grp')]
    psum x1 -> x0, waiting for transfers between devices: 53.3 us -> none  [body(): lax.psum(stacked.astype(jnp.bfloat16), 'grp').astype(jnp.float32)]
    reduce_sum x0 -> x1, other arithmetic: none -> 5.41 us  [body(): jnp.sum(lax.all_gather(stacked.astype(jnp.bfloat16), 'grp'), axis=0)]
  transfers between devices with their start and end apart: 7 -> 7, of which waited for: 6 -> 6; matrix products, arithmetic and copies ran while one was open for 15% -> 14% of each run, Pallas kernels for 0% -> 0%
where the time goes in v1:
time: 394 us; the launch traced here: 392 us
  waiting for transfers between devices  200 us (51%)
  local copies, waits for them, and re-layouts  57.8 us (15%)
  starting transfers between devices  45.2 us (11%)
  matrix products  45.1 us (11%)
  other arithmetic  29.6 us (8%)
  between operations  14.3 us (4%)
    reduce_scatter x1, waiting for transfers between devices, body(): lax.psum_scatter(replica_total, 'dom', scatter_dimension=1, tiled=True)  91.6 us
    all_gather x1, waiting for transfers between devices, body(): lax.all_gather(stacked.astype(jnp.bfloat16), 'grp')  66.5 us
    unnamed x32, local copies, waits for them, and re-layouts  23.5 us
    dot_general x2, matrix products, spread_back(): jnp.dot(owners, contrib_terms.reshape(owners.shape[1], -1), precision=lax...  15 us
    all_to_all x1, waiting for transfers between devices, body(): lax.all_to_all(pack_rows(hidden_rows[0], send_rows, live_counts), 'dom',...  14.6 us
    all_to_all x1, waiting for transfers between devices, body(): lax.all_to_all(pack_rows(hidden_rows[1], send_rows, live_counts), 'dom',...  14.6 us
    gather x5, local copies, waits for them, and re-layouts, pack_rows(): picked = jnp.take(source_rows, send_rows.reshape(-1), axis=0)  13.2 us
    gather x3, local copies, waits for them, and re-layouts, aggregate(): picked = jnp.take(source, block_set.reshape(-1), axis=0)  12.5 us
  transfers between devices with their start and end apart: 7, of which 6 were waited for; matrix products, arithmetic and copies ran while one was open for 14% of the time, Pallas kernels for 0%

profile of v1, /device:TPU:2, one launch (start us, length us, event | category | flops | bytes accessed | tf_op | source)
XLA Modules:
  0.0 392.0 jit_solution(6538253695675377575)
XLA Ops:
  8.9 3.3 gather_fusion
  13.3 12.4 %all-to-all-start = ((bf16[64,8,512]{2,1,0:T(8,128)(2,1)}), bf16[64,8,512]{2,1,0:T(8,128)(2,1)}, u32[]{:S(2)}, u32[]{:S(2)}) async-start(bf16[64,8,512]{2,1,0:T(8,128)(2,1)} %bitcast_select_fusion.4), calls=%async_computation | async-start | bytes 1048576 | tf_op jit(solution)/shard_map/all_to_all | solution.py:60
  27.5 2.6 gather_fusion.2
  30.1 2.6 gather_fusion.4
  32.8 10.3 %all-to-all-done = bf16[64,8,512]{2,1,0:T(8,128)(2,1)} async-done(((bf16[64,8,512]{2,1,0:T(8,128)(2,1)}), bf16[64,8,512]{2,1,0:T(8,128)(2,1)}, u32[]{:S(2)}, u32[]{:S(2)}) %all-to-all-start) | async-done | bytes 524320 | tf_op jit(solution)/shard_map/all_to_all | solution.py:60
  45.4 4.2 %gather_fusion.1 = bf16[32,128,512]{2,1,0:T(8,128)(2,1)} fusion(bf16[12,128,512]{2,1,0:T(8,128)(2,1)} %bitcast.138, s32[1024]{0:T(1024)S(1)} %pad_clamp_fusion), kind=kCustom, calls=%fused_computation.1.clone | custom fusion | bytes 8388736 | tf_op jit(solution)/shard_map/jit(_take)/gather | solution.py:26
  49.6 2.6 broadcast_select_fusion
  53.0 3.7 multiply_convert_fusion.3
  61.8 5.9 %all-to-all-start.1 = ((bf16[64,8,512]{2,1,0:T(8,128)(2,1)}), bf16[64,8,512]{2,1,0:T(8,128)(2,1)S(1)}, u32[]{:S(2)}, u32[]{:S(2)}) async-start(bf16[64,8,512]{2,1,0:T(8,128)(2,1)} %get-tuple-element.10), calls=%async_computation.1 | async-start | bytes 1048576 | tf_op jit(solution)/shard_map/all_to_all | solution.py:67
  69.8 4.5 %convolution_bitcast_fusion.1 = f32[8,4,128,512]{2,3,1,0:T(8,128)} fusion(bf16[8,128,512,1]{2,1,3,0:T(8,128)(2,1)S(1)} %bitcast.150, bf16[1,8,4,128,128]{4,3,2,1,0:T(8,128)(2,1)S(1)} %copy-done), kind=kOutput, calls=%fused_computation.12 | convolution fusion | flops 536870912 | bytes 10485760 | tf_op jit(solution)/shard_map/bkij,bid->bkjd/dot_general | solution.py:37
  74.3 10.4 %copy.35 = f32[4,8,128,512]{3,1,2,0:T(8,128)} copy(f32[4,8,128,512]{2,3,1,0:T(8,128)} %bitcast.127) | data formatting | bytes 16777216
  84.7 7.5 %fusion.22 = f32[8,65536]{1,0:T(8,128)} fusion(f32[32,65536]{1,0:T(8,128)} %bitcast.130, s32[32]{0:T(128)S(1)} %reshape_squeeze.5), kind=kOutput, calls=%fused_computation.67 | convolution fusion | flops 201326848 | bytes 10485888 | tf_op jit(solution)/shard_map/dot_general | solution.py:43
  92.2 3.3 reshape.174
  95.5 10.1 %all-to-all-start.2 = ((bf16[64,8,512]{2,1,0:T(8,128)(2,1)}), bf16[64,8,512]{2,1,0:T(8,128)(2,1)S(1)}, u32[]{:S(2)}, u32[]{:S(2)}) async-start(bf16[64,8,512]{2,1,0:T(8,128)(2,1)} %get-tuple-element.11), calls=%async_computation.2 | async-start | bytes 1048576 | tf_op jit(solution)/shard_map/all_to_all | solution.py:74
  107.2 4.2 %gather_fusion.3 = bf16[32,128,512]{2,1,0:T(8,128)(2,1)} fusion(bf16[12,128,512]{2,1,0:T(8,128)(2,1)} %bitcast.136, s32[1024]{0:T(1024)S(1)} %pad_clamp_fusion), kind=kCustom, calls=%fused_computation.6.clone | custom fusion | bytes 8388736 | tf_op jit(solution)/shard_map/jit(_take)/gather | solution.py:26
  111.4 2.6 broadcast_select_fusion.1
  124.6 4.2 %gather_fusion.5 = bf16[32,128,512]{2,1,0:T(8,128)(2,1)} fusion(bf16[12,128,512]{2,1,0:T(8,128)(2,1)} %bitcast.137, s32[1024]{0:T(1024)S(1)} %pad_clamp_fusion), kind=kCustom, calls=%fused_computation.7.clone | custom fusion | bytes 8388736 | tf_op jit(solution)/shard_map/jit(_take)/gather | solution.py:26
  128.7 2.6 broadcast_select_fusion.2
  134.3 4.5 %convolution_bitcast_fusion = f32[8,4,128,512]{2,3,1,0:T(8,128)} fusion(bf16[8,128,512,1]{2,1,3,0:T(8,128)(2,1)S(1)} %bitcast.149, bf16[1,8,4,128,128]{4,3,2,1,0:T(8,128)(2,1)S(1)} %copy-done), kind=kOutput, calls=%fused_computation.11 | convolution fusion | flops 536870912 | bytes 10485760 | tf_op jit(solution)/shard_map/bkij,bid->bkjd/dot_general | solution.py:37
  138.9 10.4 %copy.36 = f32[4,8,128,512]{3,1,2,0:T(8,128)} copy(f32[4,8,128,512]{2,3,1,0:T(8,128)} %bitcast.128) | data formatting | bytes 16777216
  149.2 7.5 %fusion.21 = f32[8,65536]{1,0:T(8,128)} fusion(f32[32,65536]{1,0:T(8,128)} %bitcast.129, s32[32]{0:T(128)S(1)} %reshape_squeeze.5), kind=kOutput, calls=%fused_computation.66 | convolution fusion | flops 201326848 | bytes 10485888 | tf_op jit(solution)/shard_map/dot_general | solution.py:43
  156.8 3.4 reshape.177
  160.2 3.5 convolution_bitcast_fusion.4
  165.6 66.5 %all-gather.2.cloned.1.call-done = bf16[4,3,512,512]{3,2,1,0:T(8,128)(2,1)} async-done(((bf16[1,3,512,512]{3,2,1,0:T(8,128)(2,1)}), bf16[4,3,512,512]{3,2,1,0:T(8,128)(2,1)}) %all-gather.2.cloned.1.call-update) | async-done | bytes 6291472 | tf_op jit(solution)/shard_map/all_gather | solution.py:138
  232.1 5.4 %reduce_sum.12 = bf16[3,512,512]{2,1,0:T(8,128)(2,1)} reduce(bf16[4,3,512,512]{3,2,1,0:T(8,128)(2,1)} %all-gather.2.cloned.1.call-done, bf16[]{:T(256)} %constant.19.clone.1), dimensions={0}, to_apply=%region_0.3 | reduce | flops 2359296 | bytes 7864322 | tf_op jit(solution)/shard_map/reduce_sum | solution.py:138
  237.5 3.5 convert_element_type.87
  241.0 10.5 %all-to-all-start.3 = ((bf16[64,8,512]{2,1,0:T(8,128)(2,1)}), bf16[64,8,512]{2,1,0:T(8,128)(2,1)S(1)}, u32[]{:S(2)}, u32[]{:S(2)}) async-start(bf16[64,8,512]{2,1,0:T(8,128)(2,1)} %get-tuple-element.9), calls=%async_computation.3 | async-start | bytes 1048576 | tf_op jit(solution)/shard_map/all_to_all | solution.py:101
  254.5 14.6 %all-to-all-done.3 = bf16[64,8,512]{2,1,0:T(8,128)(2,1)S(1)} async-done(((bf16[64,8,512]{2,1,0:T(8,128)(2,1)}), bf16[64,8,512]{2,1,0:T(8,128)(2,1)S(1)}, u32[]{:S(2)}, u32[]{:S(2)}) %all-to-all-start.3) | async-done | bytes 524320 | tf_op jit(solution)/shard_map/all_to_all | solution.py:101
  269.1 5.8 %all-to-all-start.4 = ((bf16[64,8,512]{2,1,0:T(8,128)(2,1)}), bf16[64,8,512]{2,1,0:T(8,128)(2,1)S(1)}, u32[]{:S(2)}, u32[]{:S(2)}) async-start(bf16[64,8,512]{2,1,0:T(8,128)(2,1)} %bitcast_select_fusion), calls=%async_computation.4 | async-start | bytes 1048576 | tf_op jit(solution)/shard_map/all_to_all | solution.py:108
  274.9 3.1 fusion.1
  278.0 14.6 %all-to-all-done.4 = bf16[64,8,512]{2,1,0:T(8,128)(2,1)S(1)} async-done(((bf16[64,8,512]{2,1,0:T(8,128)(2,1)}), bf16[64,8,512]{2,1,0:T(8,128)(2,1)S(1)}, u32[]{:S(2)}, u32[]{:S(2)}) %all-to-all-start.4) | async-done | bytes 524320 | tf_op jit(solution)/shard_map/all_to_all | solution.py:108
  293.6 91.6 %reduce-scatter.2.cloned.1.call-done = f32[3,8,512]{2,1,0:T(8,128)} async-done(((f32[3,512,512]{2,1,0:T(8,128)}), f32[3,8,512]{2,1,0:T(8,128)}) %reduce-scatter.2.cloned.1.call-update) | async-done | bytes 49168 | tf_op jit(solution)/shard_map/reduce_scatter | solution.py:141
  (64 shorter events, 35.8 us)
Async XLA Ops:
  7.2 45.1 %copy-start = (bf16[1,8,4,128,128]{4,3,2,1,0:T(8,128)(2,1)S(1)}, bf16[1,8,4,128,128]{4,3,2,1,0:T(8,128)(2,1)}, u32[]{:S(2)}) copy-start(bf16[1,8,4,128,128]{4,3,2,1,0:T(8,128)(2,1)} %param.14) | copy-start | bytes 3145732
  12.3 13.4 %copy-start.11 = (s32[1,8,4]{1,2,0:T(4,128)S(1)}, s32[1,8,4]{1,2,0:T(4,128)}, u32[]{:S(2)}) copy-start(s32[1,8,4]{1,2,0:T(4,128)} %param.15) | copy-start | bytes 388
  13.3 29.8 %all-to-all-start = ((bf16[64,8,512]{2,1,0:T(8,128)(2,1)}), bf16[64,8,512]{2,1,0:T(8,128)(2,1)}, u32[]{:S(2)}, u32[]{:S(2)}) async-start(bf16[64,8,512]{2,1,0:T(8,128)(2,1)} %bitcast_select_fusion.4), calls=%async_computation | async-start | bytes 1048576 | tf_op jit(solution)/shard_map/all_to_all | solution.py:60
  30.1 13.0 %copy-start.1 = (bf16[1,1024,512]{2,1,0:T(8,128)(2,1)S(1)}, bf16[1,1024,512]{2,1,0:T(8,128)(2,1)}, u32[]{:S(2)}) copy-start(bf16[1,1024,512]{2,1,0:T(8,128)(2,1)} %param.12) | copy-start | bytes 3145732
  53.0 3.7 copy-start.5
  56.7 2.6 copy-start.3
  56.7 2.6 copy-start.4
  61.8 33.8 %all-to-all-start.1 = ((bf16[64,8,512]{2,1,0:T(8,128)(2,1)}), bf16[64,8,512]{2,1,0:T(8,128)(2,1)S(1)}, u32[]{:S(2)}, u32[]{:S(2)}) async-start(bf16[64,8,512]{2,1,0:T(8,128)(2,1)} %get-tuple-element.10), calls=%async_computation.1 | async-start | bytes 1048576 | tf_op jit(solution)/shard_map/all_to_all | solution.py:67
  95.5 27.8 %all-to-all-start.2 = ((bf16[64,8,512]{2,1,0:T(8,128)(2,1)}), bf16[64,8,512]{2,1,0:T(8,128)(2,1)S(1)}, u32[]{:S(2)}, u32[]{:S(2)}) async-start(bf16[64,8,512]{2,1,0:T(8,128)(2,1)} %get-tuple-element.11), calls=%async_computation.2 | async-start | bytes 1048576 | tf_op jit(solution)/shard_map/all_to_all | solution.py:74
  105.7 126.4 %all-gather.2.cloned.1.call-start = ((), (), s32[]{:S(2)}) async-start(), calls=%async_computation.6 | async-start | bytes 7864320 | tf_op jit(solution)/shard_map/all_gather | solution.py:138
  114.0 1.6 copy-start.2
  114.0 2.0 copy-start.12
  131.4 1.2 copy-start.13
  132.2 2.2 copy-start.7
  132.6 1.7 copy-start.8
  156.8 3.4 copy-start.6
  160.2 3.5 copy-start.9
  160.2 3.5 copy-start.10
  165.3 219.9 %reduce-scatter.2.cloned.1.call-start = ((), (), s32[]{:S(2)}) async-start(), calls=%async_computation.7 | async-start | bytes 3194880 | tf_op jit(solution)/shard_map/reduce_scatter | solution.py:141
  241.0 28.1 %all-to-all-start.3 = ((bf16[64,8,512]{2,1,0:T(8,128)(2,1)}), bf16[64,8,512]{2,1,0:T(8,128)(2,1)S(1)}, u32[]{:S(2)}, u32[]{:S(2)}) async-start(bf16[64,8,512]{2,1,0:T(8,128)(2,1)} %get-tuple-element.9), calls=%async_computation.3 | async-start | bytes 1048576 | tf_op jit(solution)/shard_map/all_to_all | solution.py:101
  269.1 23.4 %all-to-all-start.4 = ((bf16[64,8,512]{2,1,0:T(8,128)(2,1)}), bf16[64,8,512]{2,1,0:T(8,128)(2,1)S(1)}, u32[]{:S(2)}, u32[]{:S(2)}) async-start(bf16[64,8,512]{2,1,0:T(8,128)(2,1)} %bitcast_select_fusion), calls=%async_computation.4 | async-start | bytes 1048576 | tf_op jit(solution)/shard_map/all_to_all | solution.py:108
Sparse Core Ops, SparseCore 0:
  165.4 66.6 all-gather.1
  241.1 143.9 reduce-scatter.1
